TPU v7x, 512 devices: a whole 4x8x8 slice. The times are simulated.
512 devices in a mesh: dp: 8 (over y_hi, core), mp: 64 (over z, x, y_lo).
Axes of the slice: x: 4, y: 8 (y_hi: 4, y_lo: 2; y = y_hi * 2 + y_lo), z: 8, core: 2. Of those that a mesh axis runs over, the one named last changes fastest.
Arguments:
- queries: bfloat16 [65536, 768], P(('dp', 'mp')), may hold values from -30 to 30
- first_owner: int32 [65536, 1], P(('dp', 'mp')), may hold values from 0 to 63; in each aligned block of 128 rows (0 to 127, 128 to 255, ...) at most 4 rows name the same one
- first_row: int32 [65536], P(('dp', 'mp')), may hold values from 0 to 255
- tool_table: bfloat16 [16384, 768], P('mp'), may hold values from -6 to 6
- norm_gain: bfloat16 [768], replicated, may hold values from 0.25 to 1.75
- weight_in: bfloat16 [3072, 768], P('mp'), may hold values from -0.21875 to 0.21875
- bias_in: bfloat16 [3072], P('mp'), may hold values from -3 to 3
- weight_out: bfloat16 [3072, 768], P('mp'), may hold values from -0.109375 to 0.109375
- bias_out: bfloat16 [768], replicated, may hold values from -3 to 3
- tool_embeds: bfloat16 [512, 768], P('dp'), may hold values from -2 to 2
- positive: int32 [65536], P(('dp', 'mp')), may hold values from 0 to 511
Outputs:
- updated: bfloat16 [65536, 768], P(('dp', 'mp'))
- chain_loss: float32 [65536], P(('dp', 'mp'))
- query_grad: float32 [65536, 768], P(('dp', 'mp'))
- tool_grad: float32 [512, 768], P('dp')
Inputs may be any that keep to these rules, and one draw needn't show every extreme that they name: `first_owner`: among the 128 chains of one device at most 4 name the same owner, a bound that some block reaches of them.
All inputs are finite; a program needn't handle non-finite values.
Results may differ from a plain program's by a relative error of at most 0.0078.
Values may be sent and summed in bfloat16 or wider, within the bound.
A program may use at most 64 MiB of HBM per device.

v0:
```python
import jax
import jax.numpy as jnp
import numpy as np
from jax import lax
from jax.sharding import PartitionSpec as P


def from_behind(block, axis, distance):
    devices = range(lax.axis_size(axis))
    route = [((i - distance) % len(devices), i) for i in devices]
    return lax.ppermute(block, axis, route)


def layer_normed(combined, norm_gain):
    row_mean = jnp.mean(combined, axis=1, keepdims=True)
    centred = combined - row_mean
    spread = jnp.mean(centred * centred, axis=1, keepdims=True)
    return (centred * lax.rsqrt(spread + 1e-05) * norm_gain.astype(jnp.float32)[None, :]).astype(
        jnp.bfloat16
    )


def hidden_terms(pieces, normed):
    in_piece, bias_piece, out_piece = pieces
    preact = lax.dot_general(
        normed, in_piece, (((1,), (1,)), ((), ())), preferred_element_type=jnp.float32
    )
    preact = preact + bias_piece.astype(jnp.float32)[None, :]
    activated = jax.nn.gelu(preact, approximate=True).astype(jnp.bfloat16)
    return jnp.dot(activated, out_piece, preferred_element_type=jnp.float32)


def local(
    queries,
    first_owner,
    first_row,
    tool_table,
    norm_gain,
    weight_in,
    bias_in,
    weight_out,
    bias_out,
    tool_embeds,
    positive,
):
    chain_count, feature_count = queries.shape
    groups = lax.axis_size("mp")
    cycle_size = lax.axis_size("dp")
    cycle_index = lax.axis_index("dp")
    capacity = 2 * chain_count // groups
    owner_ids = first_owner[:, 0]
    owner_marks = (owner_ids[:, None] == jnp.arange(groups, dtype=jnp.int32)[None, :]).astype(
        jnp.int32
    )
    rank_in_owner = jnp.sum((jnp.cumsum(owner_marks, axis=0) - owner_marks) * owner_marks, axis=1)
    slot_index = owner_ids * capacity + rank_in_owner
    request = (
        jnp.zeros((groups * capacity,), jnp.int32)
        .at[slot_index]
        .set(first_row)
        .reshape(groups, capacity)
    )
    table_rows = jnp.take(
        tool_table, lax.all_to_all(request, "mp", split_axis=0, concat_axis=0, tiled=True), axis=0
    )
    fetched = lax.all_to_all(table_rows, "mp", split_axis=0, concat_axis=0, tiled=True)
    first_rows = fetched.reshape(groups * capacity, feature_count)[slot_index]
    combined = queries.astype(jnp.float32) + first_rows.astype(jnp.float32)
    normed = layer_normed(combined, norm_gain)
    branch_sum = hidden_terms(
        (
            lax.all_gather(weight_in, "mp", axis=0, tiled=True),
            lax.all_gather(bias_in, "mp", axis=0, tiled=True),
            lax.all_gather(weight_out, "mp", axis=0, tiled=True),
        ),
        normed,
    )
    updated = (combined + branch_sum + bias_out.astype(jnp.float32)[None, :]).astype(jnp.bfloat16)
    block_rows = tool_embeds.shape[0]
    forward_hops = cycle_size - 1
    block_list = [tool_embeds]
    offset_list = [0]
    visiting = tool_embeds
    for hop_number in range(forward_hops):
        visiting = from_behind(visiting, "dp", 1)
        block_list.append(visiting)
        offset_list.append(hop_number + 1)
    all_tools = jnp.concatenate(block_list, axis=0)
    block_owner = (cycle_index - jnp.asarray(offset_list, jnp.int32)) % cycle_size
    column_ids = (
        block_owner[:, None] * block_rows + jnp.arange(block_rows, dtype=jnp.int32)[None, :]
    ).reshape(-1)
    scores = lax.dot_general(
        updated, all_tools, (((1,), (1,)), ((), ())), preferred_element_type=jnp.float32
    )
    row_max = jnp.max(scores, axis=1, keepdims=True)
    log_total = row_max + jnp.log(jnp.sum(jnp.exp(scores - row_max), axis=1, keepdims=True))
    is_positive = (column_ids[None, :] == positive[:, None]).astype(jnp.float32)
    chain_loss = log_total[:, 0] - jnp.sum(scores * is_positive, axis=1)
    weights_grad = (jnp.exp(scores - log_total) - is_positive).astype(jnp.bfloat16)
    query_grad = jnp.dot(weights_grad, all_tools, preferred_element_type=jnp.float32)
    position_of = np.zeros((cycle_size,), np.int32)
    for list_index, offset_value in enumerate(offset_list):
        position_of[offset_value] = list_index

    def block_term(offset_value):
        list_index = int(position_of[offset_value])
        columns = weights_grad[:, list_index * block_rows : (list_index + 1) * block_rows]
        return lax.dot_general(
            columns, updated, (((0,), (0,)), ((), ())), preferred_element_type=jnp.float32
        )

    partial_grad = jnp.zeros((block_rows, feature_count), jnp.float32)
    for hop_number in range(cycle_size - 1):
        partial_grad = partial_grad + block_term(hop_number + 1)
        partial_grad = from_behind(partial_grad.astype(jnp.bfloat16), "dp", 1).astype(
            partial_grad.dtype
        )
    partial_grad = partial_grad + block_term(0)
    grad_scale = (block_rows * cycle_size / (chain_count * groups * cycle_size)) ** 0.5
    tool_grad = lax.psum(partial_grad, "mp") * grad_scale
    return (updated, chain_loss, query_grad, tool_grad)


def solution(mesh):
    in_specs = (
        P(("dp", "mp"), None),
        P(("dp", "mp"), None),
        P(("dp", "mp")),
        P("mp", None),
        P(),
        P("mp", None),
        P("mp"),
        P("mp", None),
        P(),
        P("dp", None),
        P(("dp", "mp")),
    )
    out_specs = (P(("dp", "mp"), None), P(("dp", "mp")), P(("dp", "mp"), None), P("dp", None))
    return jax.shard_map(local, mesh=mesh, in_specs=in_specs, out_specs=out_specs, check_vma=False)
```

profile of v0, /device:TPU:16, one launch (start us, length us, event | category | flops | bytes accessed | tf_op | source)
XLA Modules:
  0.0 1266.2 jit_solution(13888815105655201328)
XLA Ops:
  8.0 0.7 all-gather.5.cloned.1.call-update
  8.7 0.7 fusion.20
  9.6 0.8 select_reduce_fusion
  11.1 1.1 scatter_custom_fusion
  12.2 0.7 all_to_all.13
  12.9 14.8 %all-to-all-start = ((s32[64,1,4]{2,1,0:T(1,128)}), s32[64,1,4]{2,1,0:T(1,128)S(1)}, u32[]{:S(2)}, u32[]{:S(2)}) async-start(s32[64,1,4]{2,1,0:T(1,128)} %bitcast.3), calls=%async_computation | async-start | bytes 65536 | tf_op jit(solution)/shard_map/all_to_all | solution.py:64
  27.7 1.9 collective-permute-start
  29.7 1.3 dynamic-slice
  31.6 0.9 dynamic-update-slice
  32.5 0.9 constant_dynamic-update-slice_fusion.7
  33.4 163.7 %all-reduce = bf16[3072]{0:T(1024)(128)(2,1)S(1)} all-reduce(bf16[3072]{0:T(1024)(128)(2,1)S(1)} %dynamic-update-slice), channel_id=1, replica_groups=mesh['dp'=8,'mp'=64] {'mp'}, use_global_device_ids=true, to_apply=%add | all-reduce | flops 3072 | bytes 12288
  198.8 1.2 gather_fusion
  200.1 1.0 broadcast_select_fusion
  201.1 5.3 all-to-all-start.1
  206.5 1.9 collective-permute-start.1
  208.5 6.4 collective-permute-done.1
  214.9 2.1 collective-permute-start.2
  217.0 7.5 collective-permute-done.2
  224.4 1.9 collective-permute-start.3
  226.4 6.5 collective-permute-done.3
  232.9 1.9 collective-permute-start.4
  234.8 5.5 collective-permute-done.4
  240.3 4.1 collective-permute-start.5
  244.4 4.4 collective-permute-done.5
  248.8 3.8 collective-permute-start.6
  252.7 5.0 collective-permute-done.6
  257.8 0.9 gather_fusion.1
  259.1 72.0 %all-gather.3.cloned.1.call-done = bf16[3072,768]{1,0:T(8,128)(2,1)} async-done(((bf16[48,768]{1,0:T(8,128)(2,1)}), bf16[3072,768]{1,0:T(8,128)(2,1)}) %all-gather.3.cloned.1.call-update) | async-done | bytes 4718608 | tf_op jit(solution)/shard_map/all_gather | solution.py:72
  331.1 314.4 %all-gather.5.cloned.1.call-done = bf16[3072,768]{1,0:T(8,128)(2,1)} async-done(((bf16[48,768]{1,0:T(8,128)(2,1)}), bf16[3072,768]{1,0:T(8,128)(2,1)}) %all-gather.5.cloned.1.call-update) | async-done | bytes 4718608 | tf_op jit(solution)/shard_map/all_gather | solution.py:74
  645.5 6.2 fusion.9
  653.4 1.9 collective-permute-start.7
  655.3 5.7 collective-permute-done.7
  661.2 1.9 collective-permute-start.8
  663.4 5.7 collective-permute-done.8
  669.1 1.9 collective-permute-start.9
  671.2 5.8 collective-permute-done.9
  677.0 1.9 collective-permute-start.10
  679.2 5.7 collective-permute-done.10
  684.9 2.1 collective-permute-start.11
  687.2 4.6 collective-permute-done.11
  691.8 3.3 collective-permute-start.12
  695.3 3.3 collective-permute-done.12
  698.6 4.5 collective-permute-start.13
  703.3 2.2 collective-permute-done.13
  705.5 0.7 convert_add_fusion.3
  706.2 1.0 fusion.49
  707.2 550.8 %all-reduce.3.cloned.1.call-done = f32[64,768]{1,0:T(8,128)} async-done(((f32[64,768]{1,0:T(8,128)}), f32[64,768]{1,0:T(8,128)}) %all-reduce.3.cloned.1.call-update) | async-done | bytes 196624 | tf_op jit(solution)/shard_map/psum | solution.py:121
  1258.0 1.6 broadcast_multiply_fusion
  (60 shorter events, 7.2 us)
Async XLA Ops:
  7.2 191.6 %copy-start = (bf16[256,768]{1,0:T(8,128)(2,1)S(1)}, bf16[256,768]{1,0:T(8,128)(2,1)}, u32[]{:S(2)}) copy-start(bf16[256,768]{1,0:T(8,128)(2,1)} %param.15) | copy-start | bytes 1179652
  7.2 323.9 %all-gather.3.cloned.1.call-start = ((), (), s32[]{:S(2)}) async-start(), calls=%async_computation.2 | async-start | bytes 4792320 | tf_op jit(solution)/shard_map/all_gather | solution.py:72
  7.9 637.6 %all-gather.5.cloned.1.call-start = ((), (), s32[]{:S(2)}) async-start(), calls=%async_computation.3 | async-start | bytes 4792320 | tf_op jit(solution)/shard_map/all_gather | solution.py:74
  12.9 185.7 %all-to-all-start = ((s32[64,1,4]{2,1,0:T(1,128)}), s32[64,1,4]{2,1,0:T(1,128)S(1)}, u32[]{:S(2)}, u32[]{:S(2)}) async-start(s32[64,1,4]{2,1,0:T(1,128)} %bitcast.3), calls=%async_computation | async-start | bytes 65536 | tf_op jit(solution)/shard_map/all_to_all | solution.py:64
  27.7 178.8 %collective-permute-start = (bf16[64,768]{1,0:T(8,128)(2,1)}, bf16[64,768]{1,0:T(8,128)(2,1)S(1)}, u32[]{:S(2)}, u32[]{:S(2)}) collective-permute-start(bf16[64,768]{1,0:T(8,128)(2,1)} %param.21), channel_id=1, source_target_pairs={{448,0},{0,64},{64,128},{128,192},{192,256},{256,320},{320,384},{3... | collective-permute-start | bytes 294920 | tf_op jit(solution)/shard_map/ppermute | solution.py:11
  201.1 56.6 %all-to-all-start.1 = ((bf16[64,4,768]{2,1,0:T(4,128)(2,1)}), bf16[64,4,768]{2,1,0:T(4,128)(2,1)S(1)}, u32[]{:S(2)}, u32[]{:S(2)}) async-start(bf16[64,4,768]{2,1,0:T(4,128)(2,1)} %broadcast_select_fusion), calls=%async_computation.1 | async-start | bytes 786432 | tf_op jit(solution)/shard_map/all_to_all | solution.py:66
  206.5 1051.5 %all-reduce.3.cloned.1.call-start = ((), (), s32[]{:S(2)}) async-start(), calls=%async_computation.4 | async-start | bytes 393216 | tf_op jit(solution)/shard_map/psum | solution.py:121
  206.5 8.4 collective-permute-start.1
  214.9 9.5 collective-permute-start.2
  224.4 8.4 collective-permute-start.3
  232.9 7.4 collective-permute-start.4
  234.8 23.9 %copy-start.2 = (bf16[128,768]{1,0:T(8,128)(2,1)S(1)}, bf16[128,768]{1,0:T(8,128)(2,1)}, u32[]{:S(2)}) copy-start(bf16[128,768]{1,0:T(8,128)(2,1)} %param.12) | copy-start | bytes 589828
  240.3 8.5 collective-permute-start.5
  248.8 8.9 collective-permute-start.6
  259.0 393.2 %copy-start.3 = (s32[128]{0:T(128)S(1)}, s32[128]{0:T(128)}, u32[]{:S(2)}) copy-start(s32[128]{0:T(128)} %param.22) | copy-start | bytes 1540
  651.7 51.4 %copy-start.1 = (bf16[128,768]{1,0:T(8,128)(2,1)}, bf16[128,768]{1,0:T(8,128)(2,1)S(1)}, u32[]{:S(2)}) copy-start(bf16[128,768]{1,0:T(8,128)(2,1)S(1)} %fusion.9) | copy-start | bytes 589828
  653.4 7.6 collective-permute-start.7
  661.2 7.9 collective-permute-start.8
  669.1 7.9 collective-permute-start.9
  677.0 7.9 collective-permute-start.10
  684.9 6.8 collective-permute-start.11
  691.8 6.8 collective-permute-start.12
  698.6 6.8 collective-permute-start.13
Sparse Core Ops, SparseCore 0:
  10.1 320.9 all-gather.2
  333.2 312.3 all-gather.4
  706.3 551.6 all-reduce.2
where the time goes:
time: 1270 us
  waiting for transfers between devices  1010 us (80%)
  blocking collectives  164 us (13%)
  starting transfers between devices  55.3 us (4%)
  between operations  14.9 us (1%)
    psum x1, waiting for transfers between devices, local(): tool_grad = lax.psum(partial_grad, 'mp') * grad_scale  551 us
    all_gather x1, waiting for transfers between devices, local(): lax.all_gather(weight_out, 'mp', axis=0, tiled=True)  314 us
    unnamed x1, blocking collectives  164 us
    all_gather x1, waiting for transfers between devices, local(): lax.all_gather(weight_in, 'mp', axis=0, tiled=True)  72 us
    ppermute x14, waiting for transfers between devices, from_behind(): return lax.ppermute(block, axis, route)  68.2 us
    ppermute x14, starting transfers between devices, from_behind(): return lax.ppermute(block, axis, route)  35.1 us
  transfers between devices with their start and end apart: 19, of which 16 were waited for; matrix products, arithmetic and copies ran while one was open for 1% of the time, Pallas kernels for 0%

commit v1 on v0

--- a/solution.py
+++ b/solution.py
@@ -118,7 +118,7 @@
         )
     partial_grad = partial_grad + block_term(0)
     grad_scale = (block_rows * cycle_size / (chain_count * groups * cycle_size)) ** 0.5
-    tool_grad = lax.psum(partial_grad, "mp") * grad_scale
+    tool_grad = jnp.sum(lax.all_gather(partial_grad, "mp"), axis=0) * grad_scale
     return (updated, chain_loss, query_grad, tool_grad)
 
 

time: 1270 us -> 1070 us (0.84)
  waiting for transfers between devices: 1010 us -> 804 us
    psum x1 -> x0, waiting for transfers between devices: 551 us -> none  [local(): tool_grad = lax.psum(partial_grad, 'mp') * grad_scale]
    all_gather x0 -> x1, waiting for transfers between devices: none -> 350 us  [local(): tool_grad = jnp.sum(lax.all_gather(partial_grad, 'mp'), axis=0) * grad_scale]
where the time goes in v1:
time: 1070 us
  waiting for transfers between devices  804 us (75%)
  blocking collectives  164 us (15%)
  starting transfers between devices  57.2 us (5%)
  between operations  14.8 us (1%)
  other arithmetic  12.8 us (1%)
    all_gather x1, waiting for transfers between devices, local(): tool_grad = jnp.sum(lax.all_gather(partial_grad, 'mp'), axis=0) * grad_scale  350 us
    all_gather x1, waiting for transfers between devices, local(): lax.all_gather(weight_out, 'mp', axis=0, tiled=True)  313 us
    unnamed x1, blocking collectives  164 us
    all_gather x1, waiting for transfers between devices, local(): lax.all_gather(weight_in, 'mp', axis=0, tiled=True)  73.3 us
    ppermute x14, waiting for transfers between devices, from_behind(): return lax.ppermute(block, axis, route)  66.4 us
    ppermute x14, starting transfers between devices, from_behind(): return lax.ppermute(block, axis, route)  36.8 us
  transfers between devices with their start and end apart: 19, of which 16 were waited for; matrix products, arithmetic and copies ran while one was open for 1% of the time, Pallas kernels for 0%

profile of v1, /device:TPU:16, one launch (start us, length us, event | category | flops | bytes accessed | tf_op | source)
XLA Modules:
  0.0 1069.3 jit_solution(13411108609109826895)
XLA Ops:
  8.0 0.7 all-gather.7.cloned.1.call-update
  8.7 0.7 fusion.20
  9.6 0.8 select_reduce_fusion
  11.1 1.1 scatter_custom_fusion
  12.2 0.7 all_to_all.13
  12.9 14.8 %all-to-all-start = ((s32[64,1,4]{2,1,0:T(1,128)}), s32[64,1,4]{2,1,0:T(1,128)S(1)}, u32[]{:S(2)}, u32[]{:S(2)}) async-start(s32[64,1,4]{2,1,0:T(1,128)} %bitcast.3), calls=%async_computation | async-start | bytes 65536 | tf_op jit(solution)/shard_map/all_to_all | solution.py:64
  27.7 1.9 collective-permute-start
  29.7 1.3 dynamic-slice
  31.6 0.9 dynamic-update-slice
  32.5 0.9 constant_dynamic-update-slice_fusion.7
  33.4 163.7 %all-reduce = bf16[3072]{0:T(1024)(128)(2,1)S(1)} all-reduce(bf16[3072]{0:T(1024)(128)(2,1)S(1)} %dynamic-update-slice), channel_id=1, replica_groups=mesh['dp'=8,'mp'=64] {'mp'}, use_global_device_ids=true, to_apply=%add | all-reduce | flops 3072 | bytes 12288
  198.7 1.2 gather_fusion
  200.1 1.0 broadcast_select_fusion
  201.1 5.5 all-to-all-start.1
  206.6 1.9 collective-permute-start.1
  208.6 6.5 collective-permute-done.1
  215.1 1.9 collective-permute-start.2
  217.0 7.6 collective-permute-done.2
  224.7 1.9 collective-permute-start.3
  226.6 6.0 collective-permute-done.3
  232.6 2.1 collective-permute-start.4
  234.7 5.4 collective-permute-done.4
  240.1 5.1 collective-permute-start.5
  245.2 3.8 collective-permute-done.5
  249.0 4.5 collective-permute-start.6
  253.5 4.2 collective-permute-done.6
  257.8 0.9 gather_fusion.1
  259.0 73.3 %all-gather.5.cloned.1.call-done = bf16[3072,768]{1,0:T(8,128)(2,1)} async-done(((bf16[48,768]{1,0:T(8,128)(2,1)}), bf16[3072,768]{1,0:T(8,128)(2,1)}) %all-gather.5.cloned.1.call-update) | async-done | bytes 4718608 | tf_op jit(solution)/shard_map/all_gather | solution.py:72
  332.3 312.6 %all-gather.7.cloned.1.call-done = bf16[3072,768]{1,0:T(8,128)(2,1)} async-done(((bf16[48,768]{1,0:T(8,128)(2,1)}), bf16[3072,768]{1,0:T(8,128)(2,1)}) %all-gather.7.cloned.1.call-update) | async-done | bytes 4718608 | tf_op jit(solution)/shard_map/all_gather | solution.py:74
  644.9 6.2 fusion.9
  652.8 1.9 collective-permute-start.7
  654.7 5.7 collective-permute-done.7
  660.6 1.9 collective-permute-start.8
  662.8 5.7 collective-permute-done.8
  668.5 1.9 collective-permute-start.9
  670.6 5.8 collective-permute-done.9
  676.4 1.9 collective-permute-start.10
  678.6 5.7 collective-permute-done.10
  684.3 2.1 collective-permute-start.11
  686.6 4.6 collective-permute-done.11
  691.2 3.3 collective-permute-start.12
  694.7 3.3 collective-permute-done.12
  698.0 4.5 collective-permute-start.13
  702.7 2.2 collective-permute-done.13
  705.6 1.0 fusion.49
  706.6 350.3 %all-gather.9.cloned.1.call-done = f32[4096,768]{1,0:T(8,128)} async-done(((f32[64,768]{1,0:T(8,128)}), f32[4096,768]{1,0:T(8,128)}) %all-gather.9.cloned.1.call-update) | async-done | bytes 12582928 | tf_op jit(solution)/shard_map/all_gather | solution.py:121
  1056.9 5.2 reduce_sum.62
  1062.1 0.7 broadcast_multiply_fusion
  (61 shorter events, 7.8 us)
Async XLA Ops:
  7.2 191.6 %copy-start = (bf16[256,768]{1,0:T(8,128)(2,1)S(1)}, bf16[256,768]{1,0:T(8,128)(2,1)}, u32[]{:S(2)}) copy-start(bf16[256,768]{1,0:T(8,128)(2,1)} %param.15) | copy-start | bytes 1179652
  7.2 325.1 %all-gather.5.cloned.1.call-start = ((), (), s32[]{:S(2)}) async-start(), calls=%async_computation.2 | async-start | bytes 4792320 | tf_op jit(solution)/shard_map/all_gather | solution.py:72
  7.9 637.0 %all-gather.7.cloned.1.call-start = ((), (), s32[]{:S(2)}) async-start(), calls=%async_computation.3 | async-start | bytes 4792320 | tf_op jit(solution)/shard_map/all_gather | solution.py:74
  12.9 185.7 %all-to-all-start = ((s32[64,1,4]{2,1,0:T(1,128)}), s32[64,1,4]{2,1,0:T(1,128)S(1)}, u32[]{:S(2)}, u32[]{:S(2)}) async-start(s32[64,1,4]{2,1,0:T(1,128)} %bitcast.3), calls=%async_computation | async-start | bytes 65536 | tf_op jit(solution)/shard_map/all_to_all | solution.py:64
  27.7 178.9 %collective-permute-start = (bf16[64,768]{1,0:T(8,128)(2,1)}, bf16[64,768]{1,0:T(8,128)(2,1)S(1)}, u32[]{:S(2)}, u32[]{:S(2)}) collective-permute-start(bf16[64,768]{1,0:T(8,128)(2,1)} %param.21), channel_id=1, source_target_pairs={{448,0},{0,64},{64,128},{128,192},{192,256},{256,320},{320,384},{3... | collective-permute-start | bytes 294920 | tf_op jit(solution)/shard_map/ppermute | solution.py:11
  201.1 56.6 %all-to-all-start.1 = ((bf16[64,4,768]{2,1,0:T(4,128)(2,1)}), bf16[64,4,768]{2,1,0:T(4,128)(2,1)S(1)}, u32[]{:S(2)}, u32[]{:S(2)}) async-start(bf16[64,4,768]{2,1,0:T(4,128)(2,1)} %broadcast_select_fusion), calls=%async_computation.1 | async-start | bytes 786432 | tf_op jit(solution)/shard_map/all_to_all | solution.py:66
  206.6 850.3 %all-gather.9.cloned.1.call-start = ((), (), s32[]{:S(2)}) async-start(), calls=%async_computation.4 | async-start | bytes 12779520 | tf_op jit(solution)/shard_map/all_gather | solution.py:121
  206.6 8.5 collective-permute-start.1
  215.1 9.6 collective-permute-start.2
  224.7 7.9 collective-permute-start.3
  232.6 7.5 collective-permute-start.4
  234.6 24.0 %copy-start.2 = (bf16[128,768]{1,0:T(8,128)(2,1)S(1)}, bf16[128,768]{1,0:T(8,128)(2,1)}, u32[]{:S(2)}) copy-start(bf16[128,768]{1,0:T(8,128)(2,1)} %param.12) | copy-start | bytes 589828
  240.1 8.9 collective-permute-start.5
  249.0 8.7 collective-permute-start.6
  259.0 392.6 %copy-start.3 = (s32[128]{0:T(128)S(1)}, s32[128]{0:T(128)}, u32[]{:S(2)}) copy-start(s32[128]{0:T(128)} %param.22) | copy-start | bytes 1540
  651.1 51.4 %copy-start.1 = (bf16[128,768]{1,0:T(8,128)(2,1)}, bf16[128,768]{1,0:T(8,128)(2,1)S(1)}, u32[]{:S(2)}) copy-start(bf16[128,768]{1,0:T(8,128)(2,1)S(1)} %fusion.9) | copy-start | bytes 589828
  652.8 7.6 collective-permute-start.7
  660.6 7.9 collective-permute-start.8
  668.5 7.9 collective-permute-start.9
  676.4 7.9 collective-permute-start.10
  684.3 6.8 collective-permute-start.11
  691.2 6.8 collective-permute-start.12
  698.0 6.8 collective-permute-start.13
Sparse Core Ops, SparseCore 0:
  10.1 322.1 all-gather.4
  334.4 310.4 all-gather.6
  705.7 351.1 all-gather.8
